TPU v7x, 128 devices: a whole 4x4x4 slice. The times are simulated.
128 devices in a mesh: req: 8 (over x, core), mlp: 16 (over z, y).
Axes of the slice: x: 4, y: 4, z: 4, core: 2. Of those that a mesh axis runs over, the one named last changes fastest.
Arguments:
- tokens: bfloat16 [8192, 4096], P(('req', 'mlp')), may hold values from -6 to 6
- layer_norm_gain: float32 [4096], replicated, may hold values from 0.1 to 1.9
- layer_norm_bias: float32 [4096], replicated, may hold values from -2 to 2
- query_key_weight: bfloat16 [4096, 16, 768], P(None, 'mlp')
- output_weight: bfloat16 [16, 256, 4096], P('mlp'), may hold values from -0.09375 to 0.09375
- up_weight: bfloat16 [4096, 8192], P(None, 'mlp'), may hold values from -0.09375 to 0.09375
- input_bias: float32 [8192], P('mlp'), may hold values from -3 to 3
- down_weight: bfloat16 [8192, 4096], P('mlp'), may hold values from -0.0625 to 0.0625
- output_bias: float32 [4096], replicated, may hold values from -2 to 2
- input_adapter_left: bfloat16 [4096, 2048], P(None, 'mlp'), may hold values from -0.09375 to 0.09375
- query_key_value_right: bfloat16 [1024, 16, 768], P(None, 'mlp'), may hold values from -1.5 to 1.5
- up_adapter_right: bfloat16 [1024, 8192], P(None, 'mlp'), may hold values from -1.5 to 1.5
- output_adapter_left: bfloat16 [16, 256, 1024], P('mlp'), may hold values from -0.09375 to 0.09375
- down_adapter_left: bfloat16 [8192, 1024], P('mlp'), may hold values from -0.0625 to 0.0625
- output_adapter_right: bfloat16 [2048, 4096], P('mlp'), may hold values from -1 to 1
- lengths: int32 [257], replicated, may hold values from 8 to 4096, as said below
- request_adapter: int32 [257], replicated, may hold values from 0 to 63
- slot_adapter: int32 [64], P('mlp'), may hold values from 0 to 63, each once
Outputs:
- mixed: bfloat16 [8192, 4096], P(('req', 'mlp'))
Inputs may be any that keep to these rules, and one draw needn't show every extreme that they name: `lengths`: one request holds exactly 4096 tokens, every other one 8 to 24; together they hold 8192 tokens. `slot_adapter`: every adapter id stands in exactly one slot.
All inputs are finite; a program needn't handle non-finite values.
Results may differ from a plain program's by a relative error of at most 0.017.
Values may be sent and summed in bfloat16 or wider, within the bound.
A program may use at most 128 MiB of HBM per device.

v0:
```python
import math
import jax
import jax.numpy as jnp
from jax import lax
from jax.sharding import PartitionSpec as P

HEAD_SIZE = 256
ROT = 64
ADAPTER_RANK = 16
ADP_DEV = 4
EPSILON = 1e-05
NEGATIVE_FILL = -1e30


def rank_product(left_side, right_side):
    return jnp.dot(left_side, right_side, preferred_element_type=jnp.float32)


def normalize(inputs, layer_norm_gain, layer_norm_bias):
    values = inputs.astype(jnp.float32)
    center = values - jnp.mean(values, axis=1, keepdims=True)
    spread = jnp.mean(center * center, axis=1, keepdims=True)
    scaled = center * lax.rsqrt(spread + EPSILON)
    return (scaled * layer_norm_gain + layer_norm_bias).astype(jnp.bfloat16)


def token_info(lengths, request_adapter, first_row, row_count):
    endings = jnp.cumsum(lengths)
    anchors = endings - lengths
    token_index = first_row + lax.iota(jnp.int32, row_count)
    inside = anchors[None, :] <= token_index[:, None]
    request = jnp.sum(inside.astype(jnp.int32), axis=1) - 1
    request_start = jnp.max(jnp.where(inside, anchors[None, :], jnp.zeros((), jnp.int32)), axis=1)
    adapter_id = jnp.take(request_adapter, jnp.maximum(request, 0))
    return (token_index, request, token_index - request_start, adapter_id)


def rotate(matrix, position):
    row_count = matrix.shape[0]
    head_count = matrix.shape[1]
    half_rot = ROT // 2
    frequency = jnp.exp(jnp.arange(half_rot, dtype=jnp.float32) * (-2.0 * math.log(10000.0) / ROT))
    angles = position.astype(jnp.float32)[:, None] * frequency[None, :]
    cosine = jnp.cos(angles)[:, None, :]
    sine_value = jnp.sin(angles)[:, None, :]
    paired_part = matrix[:, :, :ROT].reshape(row_count, head_count, half_rot, 2)
    even_part = paired_part[:, :, :, 0]
    odd_part = paired_part[:, :, :, 1]
    turned = jnp.stack(
        [even_part * cosine - odd_part * sine_value, odd_part * cosine + even_part * sine_value],
        axis=-1,
    )
    return jnp.concatenate([turned.reshape(row_count, head_count, ROT), matrix[:, :, ROT:]], axis=2)


def slot_selector(products, chosen, adapter_id, column_count):
    row_count = products.shape[0]
    selector = (adapter_id[:, None] == chosen[None, :]).astype(jnp.float32)
    reshaped = products.reshape(row_count, chosen.shape[0], column_count)
    return jnp.sum(selector[:, :, None] * reshaped, axis=1)


def widen_rows(values, chosen, adapter_id):
    selector = adapter_id[:, None] == chosen[None, :]
    spread = jnp.where(selector[:, :, None], values[:, None, :], jnp.zeros((), values.dtype))
    return spread.reshape(values.shape[0], chosen.shape[0] * values.shape[1])


def per_device(
    tokens,
    layer_norm_gain,
    layer_norm_bias,
    query_key_weight,
    output_weight,
    up_weight,
    input_bias,
    down_weight,
    output_bias,
    input_adapter_left,
    query_key_value_right,
    up_adapter_right,
    output_adapter_left,
    down_adapter_left,
    output_adapter_right,
    lengths,
    request_adapter,
    slot_adapter,
):
    tok_dev = tokens.shape[0]
    model_width = tokens.shape[1]
    mlp_count = lax.axis_size("mlp")
    tok_grp = tok_dev * mlp_count
    group_first = lax.axis_index("req") * tok_grp
    heads_local = query_key_weight.shape[1]
    hid_local = up_weight.shape[1]
    adapter_ids = slot_adapter.shape[0] * mlp_count
    every_id = lax.iota(jnp.int32, adapter_ids)
    query_key_columns = heads_local * 3 * HEAD_SIZE
    attention_columns = heads_local * HEAD_SIZE
    query_key_rows = query_key_weight.reshape(model_width, query_key_columns)
    normed_rows = normalize(tokens, layer_norm_gain, layer_norm_bias)
    slot_portion = lax.all_gather(normed_rows, "mlp", axis=0, tiled=True)
    grouped = jnp.concatenate(
        [
            rank_product(slot_portion, query_key_rows),
            rank_product(slot_portion, up_weight),
            rank_product(slot_portion, input_adapter_left),
        ],
        axis=1,
    )
    token_index, request, position, adapter_id = token_info(
        lengths, request_adapter, group_first, tok_grp
    )
    rank_part = slot_selector(
        grouped[:, query_key_columns + hid_local :], slot_adapter, adapter_id, 2 * ADAPTER_RANK
    )
    rank_input = lax.psum(rank_part.astype(jnp.bfloat16), "mlp")
    qkv_extra = rank_product(
        widen_rows(rank_input[:, :ADAPTER_RANK], every_id, adapter_id),
        query_key_value_right.reshape(adapter_ids * ADAPTER_RANK, query_key_columns),
    )
    up_delta = rank_product(
        widen_rows(rank_input[:, ADAPTER_RANK:], every_id, adapter_id), up_adapter_right
    )
    projected_rows = (grouped[:, :query_key_columns] + qkv_extra).reshape(
        tok_grp, heads_local, 3 * HEAD_SIZE
    )
    hidden_units = jax.nn.gelu(
        grouped[:, query_key_columns : query_key_columns + hid_local] + up_delta + input_bias,
        approximate=True,
    ).astype(jnp.bfloat16)
    queries = rotate(projected_rows[:, :, :HEAD_SIZE], position).astype(jnp.bfloat16)
    key_rows = (
        rotate(projected_rows[:, :, HEAD_SIZE : 2 * HEAD_SIZE], position)
        .astype(jnp.bfloat16)
        .reshape(tok_grp, attention_columns)
    )
    value_rows = (
        projected_rows[:, :, 2 * HEAD_SIZE :]
        .astype(jnp.bfloat16)
        .reshape(tok_grp, attention_columns)
    )
    paired = jnp.stack([key_rows, value_rows])
    score_scale = HEAD_SIZE ** (-0.5)
    last_row = group_first + tok_grp - 1
    start_state = (
        jnp.full((tok_grp, heads_local), NEGATIVE_FILL, jnp.float32),
        jnp.zeros((tok_grp, heads_local), jnp.float32),
        jnp.zeros((tok_grp, heads_local, HEAD_SIZE), jnp.float32),
    )
    slot_portion = lax.all_gather(paired, "req", axis=1, tiled=True)
    offset = jnp.int32(0)
    amount = slot_portion.shape[1]
    key_index, key_request, key_position, key_adapter = token_info(
        lengths, request_adapter, offset, amount
    )
    useful = jnp.logical_and(offset <= last_row, key_request[amount - 1] >= request[0])

    def attend(current):
        running_top, running_total, running_sum = current
        part_keys = slot_portion[0].reshape(amount, heads_local, HEAD_SIZE)
        part_values = slot_portion[1].reshape(amount, heads_local, HEAD_SIZE)
        scores = (
            jnp.einsum("qhd,khd->qhk", queries, part_keys, preferred_element_type=jnp.float32)
            * score_scale
        )
        allowed = jnp.logical_and(
            key_request[None, :] == request[:, None], key_index[None, :] <= token_index[:, None]
        )[:, None, :]
        masked = jnp.where(allowed, scores, NEGATIVE_FILL)
        new_top = jnp.maximum(running_top, jnp.max(masked, axis=2))
        weights = jnp.where(allowed, jnp.exp(masked - new_top[:, :, None]), 0.0)
        new_total = jnp.sum(weights, axis=2)
        new_sum = jnp.einsum(
            "qhk,khd->qhd",
            weights.astype(jnp.bfloat16),
            part_values,
            preferred_element_type=jnp.float32,
        )
        return (new_top, new_total, new_sum)

    final_state = lax.cond(useful, attend, lambda current: current, start_state)
    attention_output = (
        (final_state[2] / final_state[1][:, :, None])
        .astype(jnp.bfloat16)
        .reshape(tok_grp, attention_columns)
    )
    output_rows = output_weight.reshape(attention_columns, model_width)
    own_ids = lax.axis_index("mlp") * ADP_DEV + lax.iota(jnp.int32, ADP_DEV)
    output_rank_rows = rank_product(
        attention_output, output_adapter_left.reshape(attention_columns, adapter_ids * ADAPTER_RANK)
    )
    down_rank_rows = rank_product(hidden_units, down_adapter_left)
    rank_part_out = jnp.concatenate(
        [
            slot_selector(output_rank_rows, every_id, adapter_id, ADAPTER_RANK),
            slot_selector(down_rank_rows, every_id, adapter_id, ADAPTER_RANK),
        ],
        axis=1,
    )
    rank_output = lax.psum(rank_part_out.astype(jnp.bfloat16), "mlp")
    rank_widened = widen_rows(rank_output, own_ids, adapter_id)
    mixed = lax.psum_scatter(
        (
            rank_product(attention_output, output_rows)
            + (
                rank_product(hidden_units, down_weight)
                + rank_product(rank_widened, output_adapter_right)
            )
        ).astype(jnp.bfloat16),
        "mlp",
        scatter_dimension=0,
        tiled=True,
    ).astype(jnp.float32)
    return (mixed + tokens.astype(jnp.float32) + output_bias).astype(jnp.bfloat16)


def solution(mesh):
    in_specs = (
        P(("req", "mlp"), None),
        P(),
        P(),
        P(None, "mlp", None),
        P("mlp", None, None),
        P(None, "mlp"),
        P("mlp"),
        P("mlp", None),
        P(),
        P(None, "mlp"),
        P(None, "mlp", None),
        P(None, "mlp"),
        P("mlp", None, None),
        P("mlp", None),
        P("mlp", None),
        P(),
        P(),
        P("mlp"),
    )
    out_specs = P(("req", "mlp"), None)
    return jax.shard_map(
        per_device, mesh=mesh, in_specs=in_specs, out_specs=out_specs, check_vma=False
    )
```

profile of v0, /device:TPU:0, one launch (start us, length us, event | category | flops | bytes accessed | tf_op | source)
XLA Modules:
  0.0 493.8 jit_solution(12925493245137740278)
XLA Ops:
  6.5 1.4 convert_reduce_fusion.1
  7.9 1.3 fusion.35
  9.3 2.1 fusion.38
  13.8 6.2 %gather_fusion = s32[1024]{0:T(1024)S(1)} fusion(s32[257]{0:T(512)} %param.36, s32[1024]{0:T(1024)S(1)} %maximum_clamp_fusion), kind=kCustom, calls=%fused_computation | custom fusion | bytes 12288 | tf_op jit(solution)/shard_map/jit(_take)/gather | solution.py:34
  20.8 64.1 %all-gather.3.cloned.1.call-done = bf16[1024,4096]{1,0:T(8,128)(2,1)} async-done(((bf16[64,4096]{1,0:T(8,128)(2,1)}), bf16[1024,4096]{1,0:T(8,128)(2,1)}) %all-gather.3.cloned.1.call-update) | async-done | bytes 8388624 | tf_op jit(solution)/shard_map/all_gather | solution.py:102
  84.9 6.3 %fusion.67 = f32[1024,128]{0,1:T(8,128)S(1)} fusion(bf16[1024,4096]{1,0:T(8,128)(2,1)} %all-gather.3.cloned.1.call-done, bf16[4096,128]{1,0:T(8,128)(2,1)S(1)} %copy-done.2), kind=kOutput, calls=%fused_computation.113 | convolution fusion | flops 1073741824 | bytes 9961472 | tf_op jit(solution)/shard_map/dot_general | solution.py:16
  92.5 80.1 %all-reduce.4.cloned.1.call-done = bf16[1024,32]{0,1:T(8,128)(2,1)} async-done(((bf16[1024,32]{0,1:T(8,128)(2,1)}), bf16[1024,32]{0,1:T(8,128)(2,1)}) %all-reduce.4.cloned.1.call-update) | async-done | bytes 65552 | tf_op jit(solution)/shard_map/psum | solution.py:117
  173.4 1.8 broadcast_select_fusion
  175.2 3.3 fusion.29
  178.5 11.0 %fusion.66 = (bf16[1024,1,768]{0,2,1:T(8,128)(2,1)S(1)}, f32[1024,1,768]{0,2,1:T(8,128)S(1)}) fusion(f32[1024,768]{0,1:T(8,128)S(1)} %fusion.29, bf16[1024,4096]{1,0:T(8,128)(2,1)} %all-gather.3.cloned.1.call-done, bf16[4096,1,768]{2,0,1:T(8,128)(2,1)} %param.23), kind=kOutput, calls=%fused_computation.112 | convolution fusion | flops 6444023808 | bytes 22544384 | tf_op jit(solution)/shard_map/dot_general | solution.py:16
  190.4 2.0 reshape.569
  192.4 1.6 fusion.63
  194.0 2.0 reshape.568
  197.0 2.2 fusion.57
  206.1 2.0 copy.47
  208.2 11.3 %fusion.68 = f32[1024,512]{1,0:T(8,128)} fusion(bf16[1024,4096]{1,0:T(8,128)(2,1)} %all-gather.3.cloned.1.call-done, bf16[4096,512]{1,0:T(8,128)(2,1)} %param.25), kind=kOutput, calls=%fused_computation.114 | convolution fusion | flops 4294967296 | bytes 14680064 | tf_op jit(solution)/shard_map/dot_general | solution.py:16
  220.6 4.5 fusion.24
  225.1 1.3 fusion.70
  226.5 2.4 fusion.16
  228.9 8.3 %fusion.69 = f32[1024,4096]{1,0:T(8,128)} fusion(bf16[1024,512]{1,0:T(8,128)(2,1)S(1)} %fusion.24, bf16[512,4096]{1,0:T(8,128)(2,1)S(1)} %copy-done.9), kind=kOutput, calls=%fused_computation.115 | convolution fusion | flops 4294967296 | bytes 22020096 | tf_op jit(solution)/shard_map/dot_general | solution.py:16
  237.2 14.0 %all-gather.5.cloned.1.call-done = bf16[2,8192,256]{1,2,0:T(8,128)(2,1)} async-done(((bf16[2,1024,256]{1,2,0:T(8,128)(2,1)}), bf16[2,8192,256]{1,2,0:T(8,128)(2,1)}) %all-gather.5.cloned.1.call-update) | async-done | bytes 8388624 | tf_op jit(solution)/shard_map/all_gather | solution.py:151
  251.2 49.0 %conditional.1 = (f32[1024,1]{0,1:T(1,128)S(1)}, f32[1024,1,256]{2,0,1:T(8,128)S(1)}) conditional(s32[]{:T(128)} %convert_element_type.83, () %tuple.13, (s32[8192]{0:T(1024)S(1)}, s32[1024]{0:T(1024)S(1)}, s32[8192]{0:T(1024)S(1)}, s32[]{:T(128)}, s32[1024]{0:T(1024)S(1)}, /*index=5*/bf16[2,8192,256]{1,2,0:T(8,128)(2,1)}, ...), branch_computations={%region_9.10_spmd, %region_10.13_spmd} | conditional | flops 8774483968 | bytes 129753136 | solution.py:182
  251.2 12.0 %copy.45 = bf16[2,8192,256]{2,1,0:T(8,128)(2,1)} copy(bf16[2,8192,256]{1,2,0:T(8,128)(2,1)} %get-tuple-element.65) | data formatting | bytes 16777216 | tf_op jit(solution)/shard_map
  263.2 10.0 %fusion = (f32[1024]{0:T(1024)S(1)}, f32[8192,1024]{1,0:T(8,128)S(1)}) fusion(s32[1024]{0:T(1024)S(1)} %broadcast_add_fusion, s32[1024]{0:T(1024)S(1)} %get-tuple-element.22, s32[8192]{0:T(1024)S(1)} %get-tuple-element.23, s32[8192]{0:T(1024)S(1)} %get-tuple-element.21, bf16[1024,1,256]{0,2,1:T(8,128)(2,1)S(1)} %copy-done.4, bf16[2,8192,256]{2,1,0:T(8,128)(2,1)} %copy.45), kind=kOutput, calls=%fused_computation.4 | convolution fusion | flops 4345297920 | bytes 38350848 | tf_op jit(solution)/shard_map/cond/branch_1_fun/qhd,khd->qhk/dot_general | solution.py:164
  273.2 14.2 %fusion.7 = f32[1024,1,256]{2,0,1:T(8,128)S(1)} fusion(bf16[2,8192,256]{2,1,0:T(8,128)(2,1)} %copy.45, f32[8192,1024]{1,0:T(8,128)S(1)} %get-tuple-element.70, f32[1024]{0:T(1024)S(1)} %broadcast_maximum_fusion, s32[1024]{0:T(1024)S(1)} %broadcast_add_fusion, s32[1024]{0:T(1024)S(1)} %get-tuple-element.22, s32[8192]{0:T(1024)S(1)} %get-tuple-element.23, ...), kind=kOutput, calls=%fused_computation.12 | convolution fusion | flops 4362076160 | bytes 38875136 | tf_op jit(solution)/shard_map/cond/branch_1_fun/qhk,khd->qhd/dot_general | solution.py:174
  287.4 12.8 %fusion.2 = f32[1024]{0:T(1024)S(1)} fusion(f32[8192,1024]{1,0:T(8,128)S(1)} %get-tuple-element.70, f32[1024]{0:T(1024)S(1)} %broadcast_maximum_fusion, s32[1024]{0:T(1024)S(1)} %broadcast_add_fusion, s32[1024]{0:T(1024)S(1)} %get-tuple-element.22, s32[8192]{0:T(1024)S(1)} %get-tuple-element.23, s32[8192]{0:T(1024)S(1)} %get-tuple-element.21), kind=kLoop, calls=%fused_computation.6 | loop fusion | flops 67107840 | bytes 33636352 | tf_op jit(solution)/shard_map/cond/branch_1_fun/reduce_sum | solution.py:173
  300.2 1.9 multiply_reduce_fusion
  302.9 8.1 %fusion.25 = f32[1024,4096]{1,0:T(8,128)} fusion(bf16[1,256,4096]{2,1,0:T(8,128)(2,1)S(1)} %copy-done, f32[1024,1,256]{2,0,1:T(8,128)S(1)} %get-tuple-element.30, f32[1024]{0:T(1024)S(1)} %bitcast.116), kind=kOutput, calls=%fused_computation.37 | convolution fusion | flops 2148007936 | bytes 19927040 | tf_op jit(solution)/shard_map/dot_general | solution.py:16
  311.0 73.2 %all-reduce.6.cloned.1.call-done = bf16[1024,32]{0,1:T(8,128)(2,1)} async-done(((bf16[1024,32]{0,1:T(8,128)(2,1)}), bf16[1024,32]{0,1:T(8,128)(2,1)}) %all-reduce.6.cloned.1.call-update) | async-done | bytes 65552 | tf_op jit(solution)/shard_map/psum | solution.py:201
  385.0 15.6 %add_convert_fusion = bf16[1024,4096]{1,0:T(8,128)(2,1)} fusion(f32[1024,4096]{1,0:T(8,128)} %fusion.25, f32[1024,4096]{1,0:T(8,128)} %fusion.69, bf16[1024,128]{0,1:T(8,128)(2,1)S(1)} %bitcast.112, bf16[128,4096]{1,0:T(8,128)(2,1)} %param.34), kind=kOutput, calls=%fused_computation.19 | convolution fusion | flops 1086324736 | bytes 43253760 | tf_op jit(solution)/shard_map/dot_general | solution.py:16
  400.7 84.6 %reduce-scatter.2.cloned.1.call-done = bf16[64,4096]{1,0:T(8,128)(2,1)} async-done(((bf16[1024,4096]{1,0:T(8,128)(2,1)}), bf16[64,4096]{1,0:T(8,128)(2,1)}) %reduce-scatter.2.cloned.1.call-update) | async-done | bytes 524304 | tf_op jit(solution)/shard_map/reduce_scatter | solution.py:203
  485.3 2.0 fusion.40
  (75 shorter events, 15.5 us)
Async XLA Ops:
  6.5 296.3 %copy-start = (bf16[1,256,4096]{2,1,0:T(8,128)(2,1)S(1)}, bf16[1,256,4096]{2,1,0:T(8,128)(2,1)}, u32[]{:S(2)}) copy-start(bf16[1,256,4096]{2,1,0:T(8,128)(2,1)} %param.24) | copy-start | bytes 6291460
  6.5 13.5 %copy-start.8 = (s32[4]{0:T(128)S(1)}, s32[4]{0:T(128)}, u32[]{:S(2)}) copy-start(s32[4]{0:T(128)} %param.37) | copy-start | bytes 52
  6.5 78.4 %copy-start.2 = (bf16[4096,128]{1,0:T(8,128)(2,1)S(1)}, bf16[4096,128]{1,0:T(8,128)(2,1)}, u32[]{:S(2)}) copy-start(bf16[4096,128]{1,0:T(8,128)(2,1)} %param.29) | copy-start | bytes 3145732
  6.5 78.4 %all-gather.3.cloned.1.call-start = ((), (), s32[]{:S(2)}) async-start(), calls=%async_computation.1 | async-start | bytes 8912896 | tf_op jit(solution)/shard_map/all_gather | solution.py:102
  11.4 161.2 %all-reduce.4.cloned.1.call-start = ((), (), s32[]{:S(2)}) async-start(), calls=%async_computation.2 | async-start | bytes 131072 | tf_op jit(solution)/shard_map/psum | solution.py:117
  91.9 159.3 %all-gather.5.cloned.1.call-start = ((), (), s32[]{:S(2)}) async-start(), calls=%async_computation.3 | async-start | bytes 9437184 | tf_op jit(solution)/shard_map/all_gather | solution.py:151
  202.1 182.1 %all-reduce.6.cloned.1.call-start = ((), (), s32[]{:S(2)}) async-start(), calls=%async_computation.4 | async-start | bytes 131072 | tf_op jit(solution)/shard_map/psum | solution.py:201
  208.2 11.3 %copy-start.5 = (bf16[1024,1,32,1]{0,2,3,1:T(8,128)(2,1)S(1)}, bf16[1024,1,32,1]{0,2,3,1:T(8,128)(2,1)}, u32[]{:S(2)}) copy-start(bf16[1024,1,32,1]{0,2,3,1:T(8,128)(2,1)} %get-tuple-element.75) | copy-start | bytes 196612
  208.2 11.3 %copy-start.6 = (bf16[1024,1,32,1]{0,2,3,1:T(8,128)(2,1)S(1)}, bf16[1024,1,32,1]{0,2,3,1:T(8,128)(2,1)}, u32[]{:S(2)}) copy-start(bf16[1024,1,32,1]{0,2,3,1:T(8,128)(2,1)} %get-tuple-element.76) | copy-start | bytes 196612
  208.2 12.4 %copy-start.11 = (f32[512]{0:T(512)S(1)}, f32[512]{0:T(512)}, u32[]{:S(2)}) copy-start(f32[512]{0:T(512)} %param.26) | copy-start | bytes 6148
  220.6 4.6 copy-start.10
  225.1 1.4 copy-start.3
  225.1 3.8 copy-start.9
  251.2 12.0 %copy-start.4 = (bf16[1024,1,256]{0,2,1:T(8,128)(2,1)S(1)}, bf16[1024,1,256]{0,2,1:T(8,128)(2,1)}, u32[]{:S(2)}) copy-start(bf16[1024,1,256]{0,2,1:T(8,128)(2,1)} %get-tuple-element.66) | copy-start | bytes 1572868 | tf_op jit(solution)/shard_map/cond
  302.8 182.5 %reduce-scatter.2.cloned.1.call-start = ((), (), s32[]{:S(2)}) async-start(), calls=%async_computation.5 | async-start | bytes 8912896 | tf_op jit(solution)/shard_map/reduce_scatter | solution.py:203
  400.6 84.7 %copy-start.1 = (bf16[64,4096]{1,0:T(8,128)(2,1)S(1)}, bf16[64,4096]{1,0:T(8,128)(2,1)}, u32[]{:S(2)}) copy-start(bf16[64,4096]{1,0:T(8,128)(2,1)} %param.20) | copy-start | bytes 1572868
  400.6 84.7 %copy-start.7 = (f32[4096]{0:T(1024)S(1)}, f32[4096]{0:T(1024)}, u32[]{:S(2)}) copy-start(f32[4096]{0:T(1024)} %param.28) | copy-start | bytes 49156
Sparse Core Ops, SparseCore 0:
  11.5 73.3 all-gather.2
  92.0 80.5 all-reduce.3
  202.2 48.9 all-gather.4
  302.9 81.1 all-reduce.5
  400.8 84.4 reduce-scatter.1
where the time goes:
time: 495 us; the launch traced here: 494 us
  waiting for transfers between devices  316 us (64%)
  matrix products  95.9 us (19%)
  other arithmetic  34.2 us (7%)
  local copies, waits for them, and re-layouts  32.5 us (7%)
  between operations  14.7 us (3%)
    reduce_scatter x1, waiting for transfers between devices, per_device(): lax.psum_scatter((rank_product(attention_output, output_rows) + (rank_pro...  84.6 us
    psum x1, waiting for transfers between devices, per_device(): rank_input = lax.psum(rank_part.astype(jnp.bfloat16), 'mlp')  80.1 us
    psum x1, waiting for transfers between devices, per_device(): rank_output = lax.psum(rank_part_out.astype(jnp.bfloat16), 'mlp')  73.2 us
    dot_general x10, matrix products, rank_product(): return jnp.dot(left_side, right_side, preferred_element_type=jnp.float32)  71.7 us
    all_gather x1, waiting for transfers between devices, per_device(): slot_portion = lax.all_gather(normed_rows, 'mlp', axis=0, tiled=True)  64.1 us
    dot_general x1, matrix products, attend(): jnp.einsum('qhk,khd->qhd', weights.astype(jnp.bfloat16), part_values, pre...  14.2 us
    all_gather x1, waiting for transfers between devices, per_device(): slot_portion = lax.all_gather(paired, 'req', axis=1, tiled=True)  14 us
    reduce_sum x1, other arithmetic, attend(): new_total = jnp.sum(weights, axis=2)  12.8 us
  transfers between devices with their start and end apart: 5, of which 5 were waited for; matrix products, arithmetic and copies ran while one was open for 10% of the time, Pallas kernels for 0%

commit v1 on v0

--- a/solution.py
+++ b/solution.py
@@ -99,7 +99,9 @@
     attention_columns = heads_local * HEAD_SIZE
     query_key_rows = query_key_weight.reshape(model_width, query_key_columns)
     normed_rows = normalize(tokens, layer_norm_gain, layer_norm_bias)
-    slot_portion = lax.all_gather(normed_rows, "mlp", axis=0, tiled=True)
+    slot_portion = jnp.concatenate(
+        lax.all_to_all(jnp.stack([normed_rows] * lax.axis_size("mlp")), "mlp", 0, 0), axis=0
+    )
     grouped = jnp.concatenate(
         [
             rank_product(slot_portion, query_key_rows),

time: 495 us -> 558 us (1.13)
  waiting for transfers between devices: 316 us -> 366 us
  starting transfers between devices: 0.35 us -> 8.88 us
  local copies, waits for them, and re-layouts: 32.5 us -> 38.1 us
    all_to_all x0 -> x1, waiting for transfers between devices: none -> 114 us  [per_device(): lax.all_to_all(jnp.stack([normed_rows] * lax.axis_size('mlp')), 'mlp', 0, 0)]
    all_gather x1 -> x0, waiting for transfers between devices: 64.1 us -> none  [per_device(): slot_portion = lax.all_gather(normed_rows, 'mlp', axis=0, tiled=True)]
    all_to_all x0 -> x1, starting transfers between devices: none -> 8.31 us  [per_device(): lax.all_to_all(jnp.stack([normed_rows] * lax.axis_size('mlp')), 'mlp', 0, 0)]
    another operation x2 -> x3, local copies, waits for them, and re-layouts: 12.1 us -> 16.4 us
  transfers between devices with their start and end apart: 5 -> 5, of which waited for: 5 -> 5; matrix products, arithmetic and copies ran while one was open for 10% -> 9% of each run, Pallas kernels for 0% -> 0%
where the time goes in v1:
time: 558 us; the launch traced here: 557 us
  waiting for transfers between devices  366 us (66%)
  matrix products  96.8 us (17%)
  local copies, waits for them, and re-layouts  38.1 us (7%)
  other arithmetic  32.1 us (6%)
  between operations  14.7 us (3%)
  starting transfers between devices  8.88 us (2%)
    all_to_all x1, waiting for transfers between devices, per_device(): lax.all_to_all(jnp.stack([normed_rows] * lax.axis_size('mlp')), 'mlp', 0, 0)  114 us
    reduce_scatter x1, waiting for transfers between devices, per_device(): lax.psum_scatter((rank_product(attention_output, output_rows) + (rank_pro...  84.6 us
    psum x1, waiting for transfers between devices, per_device(): rank_input = lax.psum(rank_part.astype(jnp.bfloat16), 'mlp')  80.3 us
    psum x1, waiting for transfers between devices, per_device(): rank_output = lax.psum(rank_part_out.astype(jnp.bfloat16), 'mlp')  73.2 us
    dot_general x10, matrix products, rank_product(): return jnp.dot(left_side, right_side, preferred_element_type=jnp.float32)  72.6 us
    dot_general x1, matrix products, attend(): jnp.einsum('qhk,khd->qhd', weights.astype(jnp.bfloat16), part_values, pre...  14.2 us
    all_gather x1, waiting for transfers between devices, per_device(): slot_portion = lax.all_gather(paired, 'req', axis=1, tiled=True)  13.9 us
    reduce_sum x1, other arithmetic, attend(): new_total = jnp.sum(weights, axis=2)  12.8 us
  transfers between devices with their start and end apart: 5, of which 5 were waited for; matrix products, arithmetic and copies ran while one was open for 9% of the time, Pallas kernels for 0%

profile of v1, /device:TPU:0, one launch (start us, length us, event | category | flops | bytes accessed | tf_op | source)
XLA Modules:
  0.0 556.6 jit_solution(14011771622900082117)
XLA Ops:
  6.5 1.4 convert_reduce_fusion.1
  7.9 1.3 fusion.36
  10.6 4.3 stack.10
  14.9 8.3 %all-to-all-start = ((bf16[16,64,4096]{2,1,0:T(8,128)(2,1)}), bf16[16,64,4096]{2,1,0:T(8,128)(2,1)}, u32[]{:S(2)}, u32[]{:S(2)}) async-start(bf16[16,64,4096]{2,1,0:T(8,128)(2,1)} %stack.10), calls=%async_computation | async-start | bytes 16777216 | tf_op jit(solution)/shard_map/all_to_all | solution.py:103
  25.5 6.9 %gather_fusion = s32[1024]{0:T(1024)S(1)} fusion(s32[257]{0:T(512)S(1)} %copy-done.1, s32[1024]{0:T(1024)S(1)} %maximum_clamp_fusion), kind=kCustom, calls=%fused_computation | custom fusion | bytes 12288 | tf_op jit(solution)/shard_map/jit(_take)/gather | solution.py:34
  33.3 113.9 %all-to-all-done = bf16[16,64,4096]{2,1,0:T(8,128)(2,1)} async-done(((bf16[16,64,4096]{2,1,0:T(8,128)(2,1)}), bf16[16,64,4096]{2,1,0:T(8,128)(2,1)}, u32[]{:S(2)}, u32[]{:S(2)}) %all-to-all-start) | async-done | bytes 8388640 | tf_op jit(solution)/shard_map/all_to_all | solution.py:103
  147.2 7.2 %fusion.33 = bf16[1024,32]{0,1:T(8,128)(2,1)} fusion(bf16[1024,4096,1]{1,0,2:T(8,128)(2,1)} %bitcast.15, bf16[4,32,4096]{2,1,0:T(8,128)(2,1)} %bitcast.117, f32[1024,4]{0,1:T(4,128)S(1)} %get-tuple-element.92), kind=kOutput, calls=%fused_computation.51 | convolution fusion | flops 1073971200 | bytes 9519104 | tf_op jit(solution)/shard_map/dot_general | solution.py:16
  155.2 80.3 %all-reduce.4.cloned.1.call-done = bf16[1024,32]{0,1:T(8,128)(2,1)} async-done(((bf16[1024,32]{0,1:T(8,128)(2,1)}), bf16[1024,32]{0,1:T(8,128)(2,1)}) %all-reduce.4.cloned.1.call-update) | async-done | bytes 65552 | tf_op jit(solution)/shard_map/psum | solution.py:119
  236.3 1.8 broadcast_select_fusion
  238.0 3.3 fusion.29
  241.3 11.0 %fusion.67 = (bf16[1024,1,768]{0,2,1:T(8,128)(2,1)S(1)}, f32[1024,1,768]{0,2,1:T(8,128)S(1)}) fusion(f32[1024,768]{0,1:T(8,128)S(1)} %fusion.29, bf16[1024,4096]{1,0:T(8,128)(2,1)} %bitcast.13, bf16[4096,1,768]{2,0,1:T(8,128)(2,1)} %param.23), kind=kOutput, calls=%fused_computation.113 | convolution fusion | flops 6444023808 | bytes 22544384 | tf_op jit(solution)/shard_map/dot_general | solution.py:16
  253.3 2.0 reshape.573
  255.3 1.6 fusion.64
  256.9 2.0 reshape.572
  259.9 2.2 fusion.58
  269.0 2.0 copy.52
  271.1 11.4 %fusion.68 = f32[1024,512]{1,0:T(8,128)} fusion(bf16[1024,4096]{1,0:T(8,128)(2,1)} %bitcast.13, bf16[4096,512]{1,0:T(8,128)(2,1)} %param.25), kind=kOutput, calls=%fused_computation.114 | convolution fusion | flops 4294967296 | bytes 14680064 | tf_op jit(solution)/shard_map/dot_general | solution.py:16
  283.5 4.5 fusion.24
  289.4 2.4 fusion.16
  291.8 8.3 %fusion.69 = f32[1024,4096]{1,0:T(8,128)} fusion(bf16[1024,512]{1,0:T(8,128)(2,1)S(1)} %fusion.24, bf16[512,4096]{1,0:T(8,128)(2,1)S(1)} %copy-done.11), kind=kOutput, calls=%fused_computation.115 | convolution fusion | flops 4294967296 | bytes 22020096 | tf_op jit(solution)/shard_map/dot_general | solution.py:16
  300.1 13.9 %all-gather.2.cloned.1.call-done = bf16[2,8192,256]{1,2,0:T(8,128)(2,1)} async-done(((bf16[2,1024,256]{1,2,0:T(8,128)(2,1)}), bf16[2,8192,256]{1,2,0:T(8,128)(2,1)}) %all-gather.2.cloned.1.call-update) | async-done | bytes 8388624 | tf_op jit(solution)/shard_map/all_gather | solution.py:153
  314.1 49.0 %conditional.1 = (f32[1024,1]{0,1:T(1,128)S(1)}, f32[1024,1,256]{2,0,1:T(8,128)S(1)}) conditional(s32[]{:T(128)} %convert_element_type.83, () %tuple.13, (s32[8192]{0:T(1024)S(1)}, s32[1024]{0:T(1024)S(1)}, s32[8192]{0:T(1024)S(1)}, s32[]{:T(128)}, s32[1024]{0:T(1024)S(1)}, /*index=5*/bf16[2,8192,256]{1,2,0:T(8,128)(2,1)}, ...), branch_computations={%region_9.10_spmd, %region_10.13_spmd} | conditional | flops 8774483968 | bytes 129753136 | solution.py:184
  314.1 12.0 %copy.50 = bf16[2,8192,256]{2,1,0:T(8,128)(2,1)} copy(bf16[2,8192,256]{1,2,0:T(8,128)(2,1)} %get-tuple-element.65) | data formatting | bytes 16777216 | tf_op jit(solution)/shard_map
  326.1 10.0 %fusion = (f32[1024]{0:T(1024)S(1)}, f32[8192,1024]{1,0:T(8,128)S(1)}) fusion(s32[1024]{0:T(1024)S(1)} %broadcast_add_fusion, s32[1024]{0:T(1024)S(1)} %get-tuple-element.22, s32[8192]{0:T(1024)S(1)} %get-tuple-element.23, s32[8192]{0:T(1024)S(1)} %get-tuple-element.21, bf16[1024,1,256]{0,2,1:T(8,128)(2,1)S(1)} %copy-done.5, bf16[2,8192,256]{2,1,0:T(8,128)(2,1)} %copy.50), kind=kOutput, calls=%fused_computation.4 | convolution fusion | flops 4345297920 | bytes 38350848 | tf_op jit(solution)/shard_map/cond/branch_1_fun/qhd,khd->qhk/dot_general | solution.py:166
  336.1 14.2 %fusion.7 = f32[1024,1,256]{2,0,1:T(8,128)S(1)} fusion(bf16[2,8192,256]{2,1,0:T(8,128)(2,1)} %copy.50, f32[8192,1024]{1,0:T(8,128)S(1)} %get-tuple-element.70, f32[1024]{0:T(1024)S(1)} %broadcast_maximum_fusion, s32[1024]{0:T(1024)S(1)} %broadcast_add_fusion, s32[1024]{0:T(1024)S(1)} %get-tuple-element.22, s32[8192]{0:T(1024)S(1)} %get-tuple-element.23, ...), kind=kOutput, calls=%fused_computation.12 | convolution fusion | flops 4362076160 | bytes 38875136 | tf_op jit(solution)/shard_map/cond/branch_1_fun/qhk,khd->qhd/dot_general | solution.py:176
  350.3 12.8 %fusion.2 = f32[1024]{0:T(1024)S(1)} fusion(f32[8192,1024]{1,0:T(8,128)S(1)} %get-tuple-element.70, f32[1024]{0:T(1024)S(1)} %broadcast_maximum_fusion, s32[1024]{0:T(1024)S(1)} %broadcast_add_fusion, s32[1024]{0:T(1024)S(1)} %get-tuple-element.22, s32[8192]{0:T(1024)S(1)} %get-tuple-element.23, s32[8192]{0:T(1024)S(1)} %get-tuple-element.21), kind=kLoop, calls=%fused_computation.6 | loop fusion | flops 67107840 | bytes 33636352 | tf_op jit(solution)/shard_map/cond/branch_1_fun/reduce_sum | solution.py:175
  363.1 1.9 multiply_reduce_fusion
  365.7 8.1 %fusion.25 = f32[1024,4096]{1,0:T(8,128)} fusion(bf16[1,256,4096]{2,1,0:T(8,128)(2,1)S(1)} %copy-done, f32[1024,1,256]{2,0,1:T(8,128)S(1)} %get-tuple-element.30, f32[1024]{0:T(1024)S(1)} %bitcast.121), kind=kOutput, calls=%fused_computation.37 | convolution fusion | flops 2148007936 | bytes 19927040 | tf_op jit(solution)/shard_map/dot_general | solution.py:16
  373.8 73.2 %all-reduce.6.cloned.1.call-done = bf16[1024,32]{0,1:T(8,128)(2,1)} async-done(((bf16[1024,32]{0,1:T(8,128)(2,1)}), bf16[1024,32]{0,1:T(8,128)(2,1)}) %all-reduce.6.cloned.1.call-update) | async-done | bytes 65552 | tf_op jit(solution)/shard_map/psum | solution.py:203
  447.9 15.6 %add_convert_fusion = bf16[1024,4096]{1,0:T(8,128)(2,1)} fusion(f32[1024,4096]{1,0:T(8,128)} %fusion.25, f32[1024,4096]{1,0:T(8,128)} %fusion.69, bf16[1024,128]{0,1:T(8,128)(2,1)S(1)} %bitcast.116, bf16[128,4096]{1,0:T(8,128)(2,1)} %param.34), kind=kOutput, calls=%fused_computation.19 | convolution fusion | flops 1086324736 | bytes 43253760 | tf_op jit(solution)/shard_map/dot_general | solution.py:16
  463.5 84.6 %reduce-scatter.2.cloned.1.call-done = bf16[64,4096]{1,0:T(8,128)(2,1)} async-done(((bf16[1024,4096]{1,0:T(8,128)(2,1)}), bf16[64,4096]{1,0:T(8,128)(2,1)}) %reduce-scatter.2.cloned.1.call-update) | async-done | bytes 524304 | tf_op jit(solution)/shard_map/reduce_scatter | solution.py:205
  548.1 2.0 fusion.41
  (79 shorter events, 17.6 us)
Async XLA Ops:
  6.5 359.2 %copy-start = (bf16[1,256,4096]{2,1,0:T(8,128)(2,1)S(1)}, bf16[1,256,4096]{2,1,0:T(8,128)(2,1)}, u32[]{:S(2)}) copy-start(bf16[1,256,4096]{2,1,0:T(8,128)(2,1)} %param.24) | copy-start | bytes 6291460
  14.9 8.4 %copy-start.9 = (s32[257]{0:T(512)S(1)}, s32[257]{0:T(512)}, u32[]{:S(2)}) copy-start(s32[257]{0:T(512)} %param.35) | copy-start | bytes 3088
  14.9 8.8 %copy-start.4 = (bf16[4096,128]{1,0:T(8,128)(2,1)S(1)}, bf16[4096,128]{1,0:T(8,128)(2,1)}, u32[]{:S(2)}) copy-start(bf16[4096,128]{1,0:T(8,128)(2,1)} %param.29) | copy-start | bytes 3145732
  14.9 10.7 %copy-start.1 = (s32[257]{0:T(512)S(1)}, s32[257]{0:T(512)}, u32[]{:S(2)}) copy-start(s32[257]{0:T(512)} %param.36) | copy-start | bytes 3088
  14.9 132.3 %all-to-all-start = ((bf16[16,64,4096]{2,1,0:T(8,128)(2,1)}), bf16[16,64,4096]{2,1,0:T(8,128)(2,1)}, u32[]{:S(2)}, u32[]{:S(2)}) async-start(bf16[16,64,4096]{2,1,0:T(8,128)(2,1)} %stack.10), calls=%async_computation | async-start | bytes 16777216 | tf_op jit(solution)/shard_map/all_to_all | solution.py:103
  23.2 9.3 %copy-start.10 = (s32[4]{0:T(128)S(1)}, s32[4]{0:T(128)}, u32[]{:S(2)}) copy-start(s32[4]{0:T(128)} %param.37) | copy-start | bytes 52
  23.2 212.3 %all-reduce.4.cloned.1.call-start = ((), (), s32[]{:S(2)}) async-start(), calls=%async_computation.2 | async-start | bytes 131072 | tf_op jit(solution)/shard_map/psum | solution.py:119
  154.4 159.7 %all-gather.2.cloned.1.call-start = ((), (), s32[]{:S(2)}) async-start(), calls=%async_computation.3 | async-start | bytes 9437184 | tf_op jit(solution)/shard_map/all_gather | solution.py:153
  265.0 182.1 %all-reduce.6.cloned.1.call-start = ((), (), s32[]{:S(2)}) async-start(), calls=%async_computation.4 | async-start | bytes 131072 | tf_op jit(solution)/shard_map/psum | solution.py:203
  271.1 11.4 %copy-start.6 = (bf16[1024,1,32,1]{0,2,3,1:T(8,128)(2,1)S(1)}, bf16[1024,1,32,1]{0,2,3,1:T(8,128)(2,1)}, u32[]{:S(2)}) copy-start(bf16[1024,1,32,1]{0,2,3,1:T(8,128)(2,1)} %get-tuple-element.75) | copy-start | bytes 196612
  271.1 11.4 %copy-start.7 = (bf16[1024,1,32,1]{0,2,3,1:T(8,128)(2,1)S(1)}, bf16[1024,1,32,1]{0,2,3,1:T(8,128)(2,1)}, u32[]{:S(2)}) copy-start(bf16[1024,1,32,1]{0,2,3,1:T(8,128)(2,1)} %get-tuple-element.76) | copy-start | bytes 196612
  271.1 12.4 %copy-start.13 = (f32[512]{0:T(512)S(1)}, f32[512]{0:T(512)}, u32[]{:S(2)}) copy-start(f32[512]{0:T(512)} %param.26) | copy-start | bytes 6148
  283.5 4.6 copy-start.12
  288.1 1.4 copy-start.3
  288.1 3.8 copy-start.11
  314.1 12.0 %copy-start.5 = (bf16[1024,1,256]{0,2,1:T(8,128)(2,1)S(1)}, bf16[1024,1,256]{0,2,1:T(8,128)(2,1)}, u32[]{:S(2)}) copy-start(bf16[1024,1,256]{0,2,1:T(8,128)(2,1)} %get-tuple-element.66) | copy-start | bytes 1572868 | tf_op jit(solution)/shard_map/cond
  365.7 182.4 %reduce-scatter.2.cloned.1.call-start = ((), (), s32[]{:S(2)}) async-start(), calls=%async_computation.5 | async-start | bytes 8912896 | tf_op jit(solution)/shard_map/reduce_scatter | solution.py:205
  463.5 84.6 %copy-start.2 = (bf16[64,4096]{1,0:T(8,128)(2,1)S(1)}, bf16[64,4096]{1,0:T(8,128)(2,1)}, u32[]{:S(2)}) copy-start(bf16[64,4096]{1,0:T(8,128)(2,1)} %param.20) | copy-start | bytes 1572868
  463.5 84.6 %copy-start.8 = (f32[4096]{0:T(1024)S(1)}, f32[4096]{0:T(1024)}, u32[]{:S(2)}) copy-start(f32[4096]{0:T(1024)} %param.28) | copy-start | bytes 49156
Sparse Core Ops, SparseCore 0:
  154.5 80.9 all-reduce.3
  265.1 48.9 all-gather.1
  365.8 81.1 all-reduce.5
  463.6 84.4 reduce-scatter.1
